TPU v7x, 32 devices: a whole 2x2x4 slice. The times are simulated.
32 devices in a mesh: seq: 4 (over y, x), exp: 8 (over z, core).
Axes of the slice: x: 2, y: 2, z: 4, core: 2. Of those that a mesh axis runs over, the one named last changes fastest.
Arguments:
- inputs: bfloat16 [4096, 4096], P(('seq', 'exp')), may hold values from -6 to 6
- queries: bfloat16 [4096, 4096], P(('seq', 'exp')), may hold values from -40 to 40
- keys: bfloat16 [4096, 4096], P(('seq', 'exp')), may hold values from -4 to 4
- values: bfloat16 [4096, 4096], P(('seq', 'exp')), may hold values from -6 to 6
- norm_gain: float32 [4096], replicated, may hold values from 0.25 to 1.75
- expert_ids: int32 [4096, 2], P(('seq', 'exp')), may hold values from 0 to 7, all different within a row; in each aligned block of 128 rows (0 to 127, 128 to 255, ...) at most 32 rows name the same one
- gate_weights: float32 [4096, 2], P(('seq', 'exp')), may hold values from 0.2 to 1
- pairs: int32 [16, 2], replicated, may hold values from 0 to 7, as said below
- w_gate: bfloat16 [8, 4096, 4096], P('exp', None, 'seq'), may hold values from -0.09375 to 0.09375
- w_up: bfloat16 [8, 4096, 4096], P('exp', None, 'seq'), may hold values from -0.09375 to 0.09375
- w_down: bfloat16 [8, 4096, 4096], P('exp', 'seq'), may hold values from -0.09375 to 0.09375
Outputs:
- output: bfloat16 [4096, 4096], P(('seq', 'exp'))
Inputs may be any that keep to these rules, and one draw needn't show every extreme that they name: `pairs`: each row is (query block, key block) with the key block from the query block - 2 to the query block; rows are distinct; every block is paired with itself; some pair has distance 2. `expert_ids`: the 2 ids of a token differ; within the 128 rows of one device every expert is named exactly 32 times.
All inputs are finite; a program needn't handle non-finite values.
Results may differ from a plain program's by a relative error of at most 0.007.
Values may be sent and summed in bfloat16 or wider, within the bound.
A program may use at most 128 MiB of HBM per device.

v0:
```python
import math
import jax
import jax.numpy as jnp
from jax import lax
from jax.sharding import PartitionSpec as P

HSZ = 128
TOP = 2
BLK = 512
DIST = 2
very_negative = -1e30
norm_epsilon = 1e-05


def from_behind(value, axis, steps):
    count = lax.axis_size(axis)
    leading, last = (max(0, -steps), min(count, count - steps))
    return lax.ppermute(value, axis, [(source, source + steps) for source in range(leading, last)])


def expert_part(flat_rows, gate_slice, up_slice, down_slice):
    gate_value = jnp.dot(flat_rows, gate_slice, preferred_element_type=jnp.float32)
    up_value = jnp.dot(flat_rows, up_slice, preferred_element_type=jnp.float32)
    hidden = (jax.nn.silu(gate_value) * up_value).astype(jnp.bfloat16)
    return jnp.dot(hidden, down_slice, preferred_element_type=jnp.float32)


def block_present(pairs, query_block, distance):
    matches = (pairs[:, 0] == query_block) & (pairs[:, 1] == query_block - distance)
    return jnp.any(matches)


def per_device(
    inputs, queries, keys, values, norm_gain, expert_ids, gate_weights, pairs, w_gate, w_up, w_down
):
    rows_dev, model_width = inputs.shape
    exp_count = lax.axis_size("exp")
    score_scale = 1.0 / math.sqrt(HSZ)
    query_run, key_run, value_run = (
        lax.all_to_all(queries, "exp", split_axis=1, concat_axis=0, tiled=True),
        lax.all_to_all(keys, "exp", split_axis=1, concat_axis=0, tiled=True),
        lax.all_to_all(values, "exp", split_axis=1, concat_axis=0, tiled=True),
    )
    run_rows, group_width = query_run.shape
    heads_dev = group_width // HSZ
    tail_rows = DIST * BLK
    keys_prev, values_prev = from_behind(
        (key_run[run_rows - tail_rows :], value_run[run_rows - tail_rows :]), "seq", 1
    )
    keys_ext = jnp.concatenate([keys_prev, key_run], 0).reshape(-1, heads_dev, HSZ)
    values_ext = jnp.concatenate([values_prev, value_run], 0).reshape(-1, heads_dev, HSZ)
    blocks_dev = run_rows // BLK
    first_block = lax.axis_index("seq") * blocks_dev
    attended_blocks = []
    for local_block in range(blocks_dev):
        query_block = first_block + local_block
        query_rows = query_run[local_block * BLK : (local_block + 1) * BLK].reshape(
            BLK, heads_dev, HSZ
        )
        present = [
            block_present(pairs, query_block, DIST - key_slot) for key_slot in range(DIST + 1)
        ]
        window_start = tail_rows + (local_block - DIST) * BLK
        window_end = window_start + (DIST + 1) * BLK
        scores = (
            jnp.einsum(
                "qhd,khd->hqk",
                query_rows,
                keys_ext[window_start:window_end],
                preferred_element_type=jnp.float32,
            )
            * score_scale
        )
        key_mask = jnp.repeat(jnp.stack(present), BLK)
        scores = jnp.where(key_mask[None, None, :], scores, very_negative)
        row_top = jnp.max(scores, axis=2, keepdims=True)
        exp_scores = jnp.exp(scores - row_top)
        denominator = jnp.sum(exp_scores, axis=2)
        weights = exp_scores.astype(jnp.bfloat16)
        summed = jnp.einsum(
            "hqk,khd->qhd",
            weights,
            values_ext[window_start:window_end],
            preferred_element_type=jnp.float32,
        )
        attended_block = (summed / jnp.transpose(denominator)[:, :, None]).astype(jnp.bfloat16)
        attended_blocks.append(attended_block.reshape(BLK, group_width))
    attended_run = jnp.concatenate(attended_blocks, 0)
    attended = lax.all_to_all(attended_run, "exp", split_axis=0, concat_axis=1, tiled=True)
    mixed_sum = inputs.astype(jnp.float32) + attended.astype(jnp.float32)
    mean_square = jnp.mean(mixed_sum * mixed_sum, axis=1, keepdims=True)
    normed = (mixed_sum * lax.rsqrt(mean_square + norm_epsilon) * norm_gain[None, :]).astype(
        jnp.bfloat16
    )
    capacity = rows_dev * TOP // exp_count
    flat_ids = expert_ids.reshape(-1)
    assignments = flat_ids.shape[0]
    id_table = (flat_ids[:, None] == jnp.arange(exp_count, dtype=jnp.int32)[None, :]).astype(
        jnp.int32
    )
    ahead_count = jnp.cumsum(id_table, axis=0) - id_table
    position = jnp.sum(ahead_count * id_table, axis=1)
    target = flat_ids * capacity + position
    source = (
        jnp.zeros((exp_count * capacity,), jnp.int32)
        .at[target]
        .set(jnp.arange(assignments, dtype=jnp.int32))
    )
    outgoing = normed[source // TOP].reshape(exp_count, capacity, model_width)
    gate_slice = w_gate[0]
    up_slice = w_up[0]
    down_slice = w_down[0]
    piece_rows = lax.all_gather(
        lax.all_to_all(outgoing, "exp", split_axis=0, concat_axis=0, tiled=True),
        "seq",
        axis=0,
        tiled=True,
    )
    flat_rows = piece_rows.reshape(-1, model_width)
    slice_parts = expert_part(flat_rows, gate_slice, up_slice, down_slice).reshape(piece_rows.shape)
    slice_total = lax.psum_scatter(
        slice_parts.astype(jnp.bfloat16), "seq", scatter_dimension=0, tiled=True
    ).astype(jnp.float32)
    expert_out = lax.all_to_all(
        slice_total.astype(jnp.bfloat16), "exp", split_axis=0, concat_axis=0, tiled=True
    ).astype(slice_total.dtype)
    gathered = expert_out.reshape(exp_count * capacity, model_width)[target].reshape(
        rows_dev, TOP, model_width
    )
    output = mixed_sum + jnp.sum(gate_weights[:, :, None] * gathered, axis=1)
    return output.astype(jnp.bfloat16)


def solution(mesh):
    in_specs = (
        P(("seq", "exp"), None),
        P(("seq", "exp"), None),
        P(("seq", "exp"), None),
        P(("seq", "exp"), None),
        P(),
        P(("seq", "exp"), None),
        P(("seq", "exp"), None),
        P(),
        P("exp", None, "seq"),
        P("exp", None, "seq"),
        P("exp", "seq", None),
    )
    out_specs = P(("seq", "exp"), None)
    return jax.shard_map(
        per_device, mesh=mesh, in_specs=in_specs, out_specs=out_specs, check_vma=False
    )
```

profile of v0, /device:TPU:0, one launch (start us, length us, event | category | flops | bytes accessed | tf_op | source)
XLA Modules:
  0.0 532.3 jit_solution(13733365971950306756)
XLA Ops:
  9.6 6.4 %all-to-all-start = ((bf16[128,8,512]{2,0,1:T(8,128)(2,1)}), bf16[128,8,512]{2,0,1:T(8,128)(2,1)S(1)}, u32[]{:S(2)}, u32[]{:S(2)}) async-start(bf16[128,8,512]{2,0,1:T(8,128)(2,1)} %copy.69), calls=%async_computation | async-start | bytes 2097152 | tf_op jit(solution)/shard_map/all_to_all | solution.py:42
  17.3 25.2 %all-to-all-done = bf16[128,8,512]{2,0,1:T(8,128)(2,1)S(1)} async-done(((bf16[128,8,512]{2,0,1:T(8,128)(2,1)}), bf16[128,8,512]{2,0,1:T(8,128)(2,1)S(1)}, u32[]{:S(2)}, u32[]{:S(2)}) %all-to-all-start) | async-done | bytes 1048608 | tf_op jit(solution)/shard_map/all_to_all | solution.py:42
  42.5 3.7 all-to-all-start.1
  46.2 2.3 copy.104
  48.5 24.2 %all-to-all-done.1 = bf16[128,8,512]{0,2,1:T(8,128)(2,1)S(1)} async-done(((bf16[128,8,512]{0,2,1:T(8,128)(2,1)}), bf16[128,8,512]{0,2,1:T(8,128)(2,1)S(1)}, u32[]{:S(2)}, u32[]{:S(2)}) %all-to-all-start.1) | async-done | bytes 1048608 | tf_op jit(solution)/shard_map/all_to_all | solution.py:41
  72.7 3.6 all-to-all-start.2
  77.7 4.4 collective-permute-start.1
  88.3 3.5 collective-permute-start
  91.8 11.0 %all-to-all-done.2 = bf16[128,8,512]{2,0,1:T(8,128)(2,1)S(1)} async-done(((bf16[128,8,512]{2,0,1:T(8,128)(2,1)}), bf16[128,8,512]{2,0,1:T(8,128)(2,1)S(1)}, u32[]{:S(2)}, u32[]{:S(2)}) %all-to-all-start.2) | async-done | bytes 1048608 | tf_op jit(solution)/shard_map/all_to_all | solution.py:40
  104.7 2.8 fusion.23
  109.1 7.3 %bitcast_reduce_fusion = (f32[4,512]{1,0:T(4,128)S(1)}, f32[4,1536,512]{2,1,0:T(8,128)}) fusion(pred[1536]{0:T(1024)(128)(4,1)S(1)} %broadcast_in_dim.46, bf16[1536,4,128]{0,2,1:T(8,128)(2,1)S(1)} %bitcast.108, bf16[512,4,128]{2,1,0:T(4,128)(2,1)} %reshape.135), kind=kOutput, calls=%fused_computation.4 | convolution fusion | flops 814741504 | bytes 14689792 | tf_op jit(solution)/shard_map/qhd,khd->hqk/dot_general | solution.py:66
  117.1 7.0 %fusion.4 = f32[4,512]{1,0:T(4,128)S(1)} fusion(f32[4,1536,512]{2,1,0:T(8,128)} %get-tuple-element.18, f32[4,512]{1,0:T(4,128)S(1)} %get-tuple-element.17, pred[1536]{0:T(1024)(128)(4,1)S(1)} %broadcast_in_dim.46), kind=kLoop, calls=%fused_computation.13 | loop fusion | flops 12580864 | bytes 12600832 | tf_op jit(solution)/shard_map/reduce_sum | solution.py:78
  124.1 2.6 collective-permute-done
  128.9 3.2 divide_convert_fusion
  132.1 3.0 bitcast_reduce_fusion.1
  135.1 3.9 fusion.2
  139.0 3.2 divide_convert_fusion.1
  143.7 4.7 all-to-all-start.3
  151.6 23.4 %all-to-all-done.3 = bf16[8,128,512]{2,1,0:T(8,128)(2,1)S(1)} async-done(((bf16[8,128,512]{2,1,0:T(8,128)(2,1)}), bf16[8,128,512]{2,1,0:T(8,128)(2,1)S(1)}, u32[]{:S(2)}, u32[]{:S(2)}) %all-to-all-start.3) | async-done | bytes 1048608 | tf_op jit(solution)/shard_map/all_to_all | solution.py:89
  176.9 3.2 gather_fusion
  180.1 53.4 %all_to_all.77 = bf16[8,32,4096]{2,1,0:T(8,128)(2,1)} all-to-all(bf16[8,32,4096]{2,1,0:T(8,128)(2,1)} %bitcast.109), channel_id=1, replica_groups=mesh['seq'=4,'exp'=8] {'exp'}, dimensions={0} | all-to-all | bytes 4194304 | tf_op jit(solution)/shard_map/all_to_all | solution.py:114
  233.6 87.5 %all-gather.2.cloned.1.call-done = bf16[32,32,4096]{2,1,0:T(8,128)(2,1)} async-done(((bf16[8,32,4096]{2,1,0:T(8,128)(2,1)}), bf16[32,32,4096]{2,1,0:T(8,128)(2,1)}) %all-gather.2.cloned.1.call-update) | async-done | bytes 8388624 | tf_op jit(solution)/shard_map/all_gather | solution.py:113
  321.1 12.8 %fusion.8 = f32[1024,1024]{1,0:T(8,128)S(1)} fusion(bf16[1024,4096]{1,0:T(8,128)(2,1)} %bitcast.128, bf16[1,4096,1024]{2,1,0:T(8,128)(2,1)} %param.20), kind=kOutput, calls=%fused_computation.17 | convolution fusion | flops 8589934592 | bytes 20971520 | tf_op jit(solution)/shard_map/dot_general | solution.py:23
  333.9 12.0 %multiply_convert_fusion = bf16[1024,1024]{1,0:T(8,128)(2,1)S(1)} fusion(f32[1024,1024]{1,0:T(8,128)S(1)} %fusion.8, bf16[1024,4096]{1,0:T(8,128)(2,1)S(1)} %bitcast.129, bf16[1,4096,1024]{2,1,0:T(8,128)(2,1)} %param.19), kind=kOutput, calls=%fused_computation.27 | convolution fusion | flops 8596226048 | bytes 23068672 | tf_op jit(solution)/shard_map/dot_general | solution.py:22
  345.9 11.0 %fusion.12 = bf16[32,32,4096]{2,1,0:T(8,128)(2,1)} fusion(bf16[32,32,1024]{2,1,0:T(8,128)(2,1)S(1)} %bitcast.130, bf16[1,1024,4096]{2,1,0:T(8,128)(2,1)S(1)} %bitcast.127), kind=kOutput, calls=%fused_computation.21 | convolution fusion | flops 8594128896 | bytes 18874368 | tf_op jit(solution)/shard_map/dot_general | solution.py:25
  356.9 86.5 %reduce-scatter.2.cloned.1.call-done = bf16[8,32,4096]{2,1,0:T(8,128)(2,1)} async-done(((bf16[32,32,4096]{2,1,0:T(8,128)(2,1)}), bf16[8,32,4096]{2,1,0:T(8,128)(2,1)}) %reduce-scatter.2.cloned.1.call-update) | async-done | bytes 2097168 | tf_op jit(solution)/shard_map/reduce_scatter | solution.py:121
  443.4 4.9 all-to-all-start.5
  448.4 48.9 %all-to-all-done.5 = bf16[8,32,4096]{2,1,0:T(8,128)(2,1)} async-done(((bf16[8,32,4096]{2,1,0:T(8,128)(2,1)}), bf16[8,32,4096]{2,1,0:T(8,128)(2,1)}, u32[]{:S(2)}, u32[]{:S(2)}) %all-to-all-start.5) | async-done | bytes 2097184 | tf_op jit(solution)/shard_map/all_to_all | solution.py:124
  497.4 4.0 bitcast_convert_fusion
  501.4 7.8 %gather_fusion.1 = f32[256,4096]{1,0:T(8,128)} fusion(f32[256,4096]{1,0:T(8,128)} %bitcast_convert_fusion, s32[1024]{0:T(1024)S(1)} %pad_clamp_fusion), kind=kCustom, calls=%fused_computation.1 | custom fusion | bytes 8389632 | tf_op jit(solution)/shard_map/gather | solution.py:127
  509.2 5.8 %reshape.142 = f32[128,2,4096]{2,1,0:T(2,128)} reshape(f32[256,4096]{1,0:T(8,128)} %gather_fusion.1) | data formatting | bytes 8388608 | tf_op jit(solution)/shard_map/reshape | solution.py:127
  515.0 8.8 %multiply_reduce_fusion = f32[128,4096]{1,0:T(8,128)S(1)} fusion(f32[128,2,4096]{2,1,0:T(2,128)} %reshape.142, f32[128,2]{1,0:T(8,128)S(1)} %copy.85), kind=kLoop, calls=%fused_computation.26 | loop fusion | flops 1572864 | bytes 6292480 | tf_op jit(solution)/shard_map/reduce_sum | solution.py:130
  (79 shorter events, 26.5 us)
Async XLA Ops:
  6.5 9.4 %copy-start.6 = (bf16[128,4096]{1,0:T(8,128)(2,1)S(1)}, bf16[128,4096]{1,0:T(8,128)(2,1)}, u32[]{:S(2)}) copy-start(bf16[128,4096]{1,0:T(8,128)(2,1)} %param.13) | copy-start | bytes 3145732
  9.6 32.9 %all-to-all-start = ((bf16[128,8,512]{2,0,1:T(8,128)(2,1)}), bf16[128,8,512]{2,0,1:T(8,128)(2,1)S(1)}, u32[]{:S(2)}, u32[]{:S(2)}) async-start(bf16[128,8,512]{2,0,1:T(8,128)(2,1)} %copy.69), calls=%async_computation | async-start | bytes 2097152 | tf_op jit(solution)/shard_map/all_to_all | solution.py:42
  42.5 39.6 %copy-start.10 = (s32[16,2]{0,1:T(2,128)S(1)}, s32[16,2]{0,1:T(2,128)}, u32[]{:S(2)}) copy-start(s32[16,2]{0,1:T(2,128)} %param.18) | copy-start | bytes 388
  42.5 30.2 %all-to-all-start.1 = ((bf16[128,8,512]{0,2,1:T(8,128)(2,1)}), bf16[128,8,512]{0,2,1:T(8,128)(2,1)S(1)}, u32[]{:S(2)}, u32[]{:S(2)}) async-start(bf16[128,8,512]{0,2,1:T(8,128)(2,1)} %bitcast.8), calls=%async_computation.1 | async-start | bytes 2097152 | tf_op jit(solution)/shard_map/all_to_all | solution.py:41
  72.7 3.6 copy-start.4
  72.7 30.1 %all-to-all-start.2 = ((bf16[128,8,512]{2,0,1:T(8,128)(2,1)}), bf16[128,8,512]{2,0,1:T(8,128)(2,1)S(1)}, u32[]{:S(2)}, u32[]{:S(2)}) async-start(bf16[128,8,512]{2,0,1:T(8,128)(2,1)} %bitcast.103), calls=%async_computation.2 | async-start | bytes 2097152 | tf_op jit(solution)/shard_map/all_to_all | solution.py:40
  77.7 26.9 %collective-permute-start.1 = (bf16[1024,512]{1,0:T(8,128)(2,1)S(1)}, bf16[1024,512]{1,0:T(8,128)(2,1)}, u32[]{:S(2)}, u32[]{:S(2)}) collective-permute-start(bf16[1024,512]{1,0:T(8,128)(2,1)S(1)} %bitcast.110), channel_id=1, source_target_pairs={{0,8},{8,16},{16,24},{1,9},{9,17},{17,25},{2,10},{10,18},{18,26},{... | collective-permute-start | bytes 3145736 | tf_op jit(solution)/shard_map/ppermute | solution.py:18
  88.3 38.4 %collective-permute-start = (bf16[1024,512]{0,1:T(8,128)(2,1)}, bf16[1024,512]{0,1:T(8,128)(2,1)}, u32[]{:S(2)}, u32[]{:S(2)}) collective-permute-start(bf16[1024,512]{0,1:T(8,128)(2,1)} %copy.70), channel_id=1, source_target_pairs={{0,8},{8,16},{16,24},{1,9},{9,17},{17,25},{2,10},{10,18},{18,26},{... | collective-permute-start | bytes 3145736 | tf_op jit(solution)/shard_map/ppermute | solution.py:18
  117.1 11.7 %copy-start = (f32[4,1536,512]{2,1,0:T(8,128)S(1)}, f32[4,1536,512]{2,1,0:T(8,128)}, u32[]{:S(2)}) copy-start(f32[4,1536,512]{2,1,0:T(8,128)} %get-tuple-element.18) | copy-start | bytes 37748740
  128.9 3.2 copy-start.5
  142.2 6.3 %copy-start.8 = (s32[128,2]{0,1:T(2,128)S(1)}, s32[128,2]{0,1:T(2,128)}, u32[]{:S(2)}) copy-start(s32[128,2]{0,1:T(2,128)} %param.16) | copy-start | bytes 3076
  143.7 31.3 %all-to-all-start.3 = ((bf16[8,128,512]{2,1,0:T(8,128)(2,1)}), bf16[8,128,512]{2,1,0:T(8,128)(2,1)S(1)}, u32[]{:S(2)}, u32[]{:S(2)}) async-start(bf16[8,128,512]{2,1,0:T(8,128)(2,1)} %bitcast.26), calls=%async_computation.3 | async-start | bytes 2097152 | tf_op jit(solution)/shard_map/all_to_all | solution.py:89
  148.4 27.1 %copy-start.1 = (bf16[128,4096]{1,0:T(8,128)(2,1)S(1)}, bf16[128,4096]{1,0:T(8,128)(2,1)}, u32[]{:S(2)}) copy-start(bf16[128,4096]{1,0:T(8,128)(2,1)} %param.11) | copy-start | bytes 3145732
  148.4 172.6 %all-gather.2.cloned.1.call-start = ((), (), s32[]{:S(2)}) async-start(), calls=%async_computation.7 | async-start | bytes 10485760 | tf_op jit(solution)/shard_map/all_gather | solution.py:113
  175.3 1.2 copy-start.2
  175.3 1.2 copy-start.7
  233.5 209.9 %reduce-scatter.2.cloned.1.call-start = ((), (), s32[]{:S(2)}) async-start(), calls=%async_computation.8 | async-start | bytes 10485760 | tf_op jit(solution)/shard_map/reduce_scatter | solution.py:121
  321.1 12.9 %copy-start.11 = (bf16[32,32,4096]{2,1,0:T(8,128)(2,1)S(1)}, bf16[32,32,4096]{2,1,0:T(8,128)(2,1)}, u32[]{:S(2)}) copy-start(bf16[32,32,4096]{2,1,0:T(8,128)(2,1)} %all-gather.2.cloned.1.call-done) | copy-start | bytes 25165828
  321.1 24.8 %slice-start = ((s8[8388608]{0:T(1024)(128)(4,1)}), s8[4194304]{0:T(1024)(128)(4,1)S(1)}, s32[]{:S(2)}) async-start(s8[8388608]{0:T(1024)(128)(4,1)} %bitcast.126), calls=%async_computation.9 | async-start | bytes 8388608
  333.9 12.0 %slice-start.1 = ((s8[8388608]{0:T(1024)(128)(4,1)}), s8[4194304]{0:T(1024)(128)(4,1)S(1)}, s32[]{:S(2)}) async-start(s8[8388608]{0:T(1024)(128)(4,1)} %bitcast.126), calls=%async_computation.10 | async-start | bytes 8388608
  356.9 91.4 %copy-start.9 = (f32[128,2]{0,1:T(2,128)S(1)}, f32[128,2]{0,1:T(2,128)}, u32[]{:S(2)}) copy-start(f32[128,2]{0,1:T(2,128)} %param.17) | copy-start | bytes 3076
  443.4 54.0 %all-to-all-start.5 = ((bf16[8,32,4096]{2,1,0:T(8,128)(2,1)}), bf16[8,32,4096]{2,1,0:T(8,128)(2,1)}, u32[]{:S(2)}, u32[]{:S(2)}) async-start(bf16[8,32,4096]{2,1,0:T(8,128)(2,1)} %reduce-scatter.2.cloned.1.call-done), calls=%async_computation.6 | async-start | bytes 4194304 | tf_op jit(solution)/shard_map/all_to_all | solution.py:124
  515.0 8.8 %copy-start.3 = (bf16[128,4096]{1,0:T(8,128)(2,1)S(1)}, bf16[128,4096]{1,0:T(8,128)(2,1)}, u32[]{:S(2)}) copy-start(bf16[128,4096]{1,0:T(8,128)(2,1)} %param.11) | copy-start | bytes 3145732
Sparse Core Ops, SparseCore 0:
  233.6 87.3 all-gather.1
  357.1 86.3 reduce-scatter.1
where the time goes:
time: 543 us; the launch traced here: 532 us
  waiting for transfers between devices  309 us (57%)
  blocking collectives  53.4 us (10%)
  matrix products  52.4 us (10%)
  other arithmetic  36.6 us (7%)
  local copies, waits for them, and re-layouts  35.4 us (7%)
  starting transfers between devices  31.2 us (6%)
  between operations  14 us (3%)
    all_gather x1, waiting for transfers between devices, per_device(): lax.all_gather(lax.all_to_all(outgoing, 'exp', split_axis=0, concat_axis=...  87.5 us
    reduce_scatter x1, waiting for transfers between devices, per_device(): lax.psum_scatter(slice_parts.astype(jnp.bfloat16), 'seq', scatter_dimensi...  86.5 us
    all_to_all x1, blocking collectives, per_device(): lax.all_to_all(outgoing, 'exp', split_axis=0, concat_axis=0, tiled=True)  53.4 us
    all_to_all x1, waiting for transfers between devices, per_device(): lax.all_to_all(slice_total.astype(jnp.bfloat16), 'exp', split_axis=0, con...  48.9 us
    all_to_all x1, waiting for transfers between devices, per_device(): lax.all_to_all(values, 'exp', split_axis=1, concat_axis=0, tiled=True)  25.2 us
    all_to_all x1, waiting for transfers between devices, per_device(): lax.all_to_all(keys, 'exp', split_axis=1, concat_axis=0, tiled=True)  24.2 us
    all_to_all x1, waiting for transfers between devices, per_device(): lax.all_to_all(attended_run, 'exp', split_axis=0, concat_axis=1, tiled=True)  23.4 us
    dot_general x1, matrix products, expert_part(): up_value = jnp.dot(flat_rows, up_slice, preferred_element_type=jnp.float32)  12.8 us
  transfers between devices with their start and end apart: 9, of which 9 were waited for; matrix products, arithmetic and copies ran while one was open for 7% of the time, Pallas kernels for 0%

commit v1 on v0

--- a/solution.py
+++ b/solution.py
@@ -10,6 +10,18 @@
 DIST = 2
 very_negative = -1e30
 norm_epsilon = 1e-05
+
+
+def exchange_directly(shard, axis, split, join):
+    ways, here = (lax.axis_size(axis), lax.axis_index(axis))
+    width = shard.shape[split] // ways
+    turned = jnp.roll(shard, -here * width, axis=split)
+    got = [lax.slice_in_dim(turned, 0, width, axis=split)]
+    for far in range(1, ways):
+        sent = lax.slice_in_dim(turned, far * width, (far + 1) * width, axis=split)
+        got.append(lax.ppermute(sent, axis, [(d, (d + far) % ways) for d in range(ways)]))
+    line = jnp.concatenate(got[::-1], axis=join)
+    return jnp.roll(line, (here + 1) * got[0].shape[join], axis=join)
 
 
 def from_behind(value, axis, steps):
@@ -38,7 +50,7 @@
     score_scale = 1.0 / math.sqrt(HSZ)
     query_run, key_run, value_run = (
         lax.all_to_all(queries, "exp", split_axis=1, concat_axis=0, tiled=True),
-        lax.all_to_all(keys, "exp", split_axis=1, concat_axis=0, tiled=True),
+        exchange_directly(keys, "exp", 1, 0),
         lax.all_to_all(values, "exp", split_axis=1, concat_axis=0, tiled=True),
     )
     run_rows, group_width = query_run.shape

time: 543 us -> 553 us (1.018)
  local copies, waits for them, and re-layouts: 35.4 us -> 51.9 us
  waiting for transfers between devices: 309 us -> 301 us
  starting transfers between devices: 31.2 us -> 39 us
    ppermute x0 -> x7, waiting for transfers between devices: none -> 36.5 us  [exchange_directly(): lax.ppermute(sent, axis, [(d, (d + far) % ways) for d in range(ways)])]
    all_to_all x1, waiting for transfers between devices: 25.2 us -> 0.01 us  [per_device(): lax.all_to_all(values, 'exp', split_axis=1, concat_axis=0, tiled=True)]
    all_to_all x1 -> x0, waiting for transfers between devices: 24.2 us -> none  [per_device(): lax.all_to_all(keys, 'exp', split_axis=1, concat_axis=0, tiled=True)]
    ppermute x2, waiting for transfers between devices: 2.61 us -> 17.8 us  [from_behind(): lax.ppermute(value, axis, [(source, source + steps) for source in range(l...]
    unnamed x32 -> x49, local copies, waits for them, and re-layouts: 3.96 us -> 17.4 us
    ppermute x0 -> x7, starting transfers between devices: none -> 11.7 us  [exchange_directly(): lax.ppermute(sent, axis, [(d, (d + far) % ways) for d in range(ways)])]
    all_to_all x1, waiting for transfers between devices: 11 us -> 0.01 us  [per_device(): lax.all_to_all(queries, 'exp', split_axis=1, concat_axis=0, tiled=True)]
  transfers between devices with their start and end apart: 9 -> 15, of which waited for: 9 -> 9; matrix products, arithmetic and copies ran while one was open for 7% -> 10% of each run, Pallas kernels for 0% -> 0%
where the time goes in v1:
time: 553 us; the launch traced here: 545 us
  waiting for transfers between devices  301 us (54%)
  blocking collectives  53.4 us (10%)
  local copies, waits for them, and re-layouts  51.9 us (9%)
  matrix products  49.1 us (9%)
  starting transfers between devices  39 us (7%)
  other arithmetic  35.8 us (6%)
  between operations  14.1 us (3%)
    all_gather x1, waiting for transfers between devices, per_device(): lax.all_gather(lax.all_to_all(outgoing, 'exp', split_axis=0, concat_axis=...  88.4 us
    reduce_scatter x1, waiting for transfers between devices, per_device(): lax.psum_scatter(slice_parts.astype(jnp.bfloat16), 'seq', scatter_dimensi...  86.5 us
    all_to_all x1, blocking collectives, per_device(): lax.all_to_all(outgoing, 'exp', split_axis=0, concat_axis=0, tiled=True)  53.4 us
    all_to_all x1, waiting for transfers between devices, per_device(): lax.all_to_all(slice_total.astype(jnp.bfloat16), 'exp', split_axis=0, con...  48.9 us
    ppermute x7, waiting for transfers between devices, exchange_directly(): lax.ppermute(sent, axis, [(d, (d + far) % ways) for d in range(ways)])  36.5 us
    all_to_all x1, waiting for transfers between devices, per_device(): lax.all_to_all(attended_run, 'exp', split_axis=0, concat_axis=1, tiled=True)  23.3 us
    ppermute x2, waiting for transfers between devices, from_behind(): lax.ppermute(value, axis, [(source, source + steps) for source in range(l...  17.8 us
    unnamed x49, local copies, waits for them, and re-layouts  17.4 us
  transfers between devices with their start and end apart: 15, of which 9 were waited for; matrix products, arithmetic and copies ran while one was open for 10% of the time, Pallas kernels for 0%

profile of v1, /device:TPU:0, one launch (start us, length us, event | category | flops | bytes accessed | tf_op | source)
XLA Modules:
  0.0 544.6 jit_solution(7281737212376796944)
XLA Ops:
  8.2 3.7 fusion.31
  12.8 4.5 collective-permute-start.1
  19.3 3.6 all-to-all-start
  22.9 3.8 collective-permute-start.2
  26.6 2.4 collective-permute-start.4
  31.9 12.1 %collective-permute-done.2 = bf16[128,512]{0,1:T(8,128)(2,1)S(1)} collective-permute-done((bf16[128,512]{0,1:T(8,128)(2,1)}, bf16[128,512]{0,1:T(8,128)(2,1)S(1)}, u32[]{:S(2)}, u32[]{:S(2)}) %collective-permute-start.2) | collective-permute-done | bytes 131104 | tf_op jit(solution)/shard_map/ppermute | solution.py:22
  47.5 22.2 %collective-permute-done.4 = bf16[128,512]{0,1:T(8,128)(2,1)} collective-permute-done((bf16[128,512]{0,1:T(8,128)(2,1)}, bf16[128,512]{0,1:T(8,128)(2,1)}, u32[]{:S(2)}, u32[]{:S(2)}) %collective-permute-start.4) | collective-permute-done | bytes 131104 | tf_op jit(solution)/shard_map/ppermute | solution.py:22
  80.8 4.4 all-to-all-start.1
  87.9 4.4 collective-permute-start.8
  97.1 17.1 %collective-permute-done.8 = bf16[1024,512]{0,1:T(8,128)(2,1)} collective-permute-done((bf16[1024,512]{0,1:T(8,128)(2,1)S(1)}, bf16[1024,512]{0,1:T(8,128)(2,1)}, u32[]{:S(2)}, u32[]{:S(2)}) %collective-permute-start.8) | collective-permute-done | bytes 1048608 | tf_op jit(solution)/shard_map/ppermute | solution.py:30
  118.6 5.5 %collective-permute-start = (bf16[1024,512]{0,1:T(8,128)(2,1)}, bf16[1024,512]{0,1:T(8,128)(2,1)}, u32[]{:S(2)}, u32[]{:S(2)}) collective-permute-start(bf16[1024,512]{0,1:T(8,128)(2,1)} %copy.51), channel_id=1, source_target_pairs={{0,8},{8,16},{16,24},{1,9},{9,17},{17,25},{2,10},{10,18},{18,26},{... | collective-permute-start | bytes 3145736 | tf_op jit(solution)/shard_map/ppermute | solution.py:30
  130.3 4.1 bitcast_reduce_fusion
  134.4 3.9 fusion.4
  138.3 3.0 bitcast_reduce_fusion.1
  141.3 3.5 fusion.2
  147.3 3.2 divide_convert_fusion
  150.4 3.2 divide_convert_fusion.1
  155.1 4.5 all-to-all-start.2
  162.9 23.3 %all-to-all-done.2 = bf16[8,128,512]{2,1,0:T(8,128)(2,1)S(1)} async-done(((bf16[8,128,512]{2,1,0:T(8,128)(2,1)}), bf16[8,128,512]{2,1,0:T(8,128)(2,1)S(1)}, u32[]{:S(2)}, u32[]{:S(2)}) %all-to-all-start.2) | async-done | bytes 1048608 | tf_op jit(solution)/shard_map/all_to_all | solution.py:101
  188.5 3.2 gather_fusion
  191.7 53.4 %all_to_all.58 = bf16[8,32,4096]{2,1,0:T(8,128)(2,1)} all-to-all(bf16[8,32,4096]{2,1,0:T(8,128)(2,1)} %bitcast.106), channel_id=1, replica_groups=mesh['seq'=4,'exp'=8] {'exp'}, dimensions={0} | all-to-all | bytes 4194304 | tf_op jit(solution)/shard_map/all_to_all | solution.py:126
  245.2 88.4 %all-gather.2.cloned.1.call-done = bf16[32,32,4096]{2,1,0:T(8,128)(2,1)} async-done(((bf16[8,32,4096]{2,1,0:T(8,128)(2,1)}), bf16[32,32,4096]{2,1,0:T(8,128)(2,1)}) %all-gather.2.cloned.1.call-update) | async-done | bytes 8388624 | tf_op jit(solution)/shard_map/all_gather | solution.py:125
  333.6 12.7 %fusion.8 = f32[1024,1024]{1,0:T(8,128)S(1)} fusion(bf16[1024,4096]{1,0:T(8,128)(2,1)} %bitcast.121, bf16[1,4096,1024]{2,1,0:T(8,128)(2,1)} %param.20), kind=kOutput, calls=%fused_computation.17 | convolution fusion | flops 8589934592 | bytes 20971520 | tf_op jit(solution)/shard_map/dot_general | solution.py:35
  346.3 12.0 %multiply_convert_fusion = bf16[1024,1024]{1,0:T(8,128)(2,1)S(1)} fusion(f32[1024,1024]{1,0:T(8,128)S(1)} %fusion.8, bf16[1024,4096]{1,0:T(8,128)(2,1)S(1)} %bitcast.122, bf16[1,4096,1024]{2,1,0:T(8,128)(2,1)} %param.19), kind=kOutput, calls=%fused_computation.27 | convolution fusion | flops 8596226048 | bytes 23068672 | tf_op jit(solution)/shard_map/dot_general | solution.py:34
  358.3 11.0 %fusion.12 = bf16[32,32,4096]{2,1,0:T(8,128)(2,1)} fusion(bf16[32,32,1024]{2,1,0:T(8,128)(2,1)S(1)} %bitcast.123, bf16[1,1024,4096]{2,1,0:T(8,128)(2,1)S(1)} %bitcast.120), kind=kOutput, calls=%fused_computation.21 | convolution fusion | flops 8594128896 | bytes 18874368 | tf_op jit(solution)/shard_map/dot_general | solution.py:37
  369.3 86.5 %reduce-scatter.2.cloned.1.call-done = bf16[8,32,4096]{2,1,0:T(8,128)(2,1)} async-done(((bf16[32,32,4096]{2,1,0:T(8,128)(2,1)}), bf16[8,32,4096]{2,1,0:T(8,128)(2,1)}) %reduce-scatter.2.cloned.1.call-update) | async-done | bytes 2097168 | tf_op jit(solution)/shard_map/reduce_scatter | solution.py:133
  455.8 4.9 all-to-all-start.4
  460.8 48.9 %all-to-all-done.4 = bf16[8,32,4096]{2,1,0:T(8,128)(2,1)} async-done(((bf16[8,32,4096]{2,1,0:T(8,128)(2,1)}), bf16[8,32,4096]{2,1,0:T(8,128)(2,1)}, u32[]{:S(2)}, u32[]{:S(2)}) %all-to-all-start.4) | async-done | bytes 2097184 | tf_op jit(solution)/shard_map/all_to_all | solution.py:136
  509.7 4.0 bitcast_convert_fusion
  513.7 7.8 %gather_fusion.1 = f32[256,4096]{1,0:T(8,128)} fusion(f32[256,4096]{1,0:T(8,128)} %bitcast_convert_fusion, s32[1024]{0:T(1024)S(1)} %pad_clamp_fusion), kind=kCustom, calls=%fused_computation.1 | custom fusion | bytes 8389632 | tf_op jit(solution)/shard_map/gather | solution.py:139
  521.6 5.8 %reshape.139 = f32[128,2,4096]{2,1,0:T(2,128)} reshape(f32[256,4096]{1,0:T(8,128)} %gather_fusion.1) | data formatting | bytes 8388608 | tf_op jit(solution)/shard_map/reshape | solution.py:139
  527.4 8.8 %multiply_reduce_fusion = f32[128,4096]{1,0:T(8,128)S(1)} fusion(f32[128,2,4096]{2,1,0:T(2,128)} %reshape.139, f32[128,2]{1,0:T(8,128)S(1)} %copy.64), kind=kLoop, calls=%fused_computation.26 | loop fusion | flops 1572864 | bytes 6292480 | tf_op jit(solution)/shard_map/reduce_sum | solution.py:142
  (109 shorter events, 51.1 us)
Async XLA Ops:
  8.2 9.2 %copy-start.6 = (bf16[128,4096]{1,0:T(8,128)(2,1)S(1)}, bf16[128,4096]{1,0:T(8,128)(2,1)}, u32[]{:S(2)}) copy-start(bf16[128,4096]{1,0:T(8,128)(2,1)} %param.14) | copy-start | bytes 3145732
  12.8 17.3 %collective-permute-start.1 = (bf16[128,512]{0,1:T(8,128)(2,1)}, bf16[128,512]{0,1:T(8,128)(2,1)S(1)}, u32[]{:S(2)}, u32[]{:S(2)}) collective-permute-start(bf16[128,512]{0,1:T(8,128)(2,1)} %get-tuple-element.23), channel_id=1, source_target_pairs={{0,7},{1,0},{2,1},{3,2},{4,3},{5,4},{6,5},{7,6},{8,15},{9,8},{10,9... | collective-permute-start | bytes 393224 | tf_op jit(solution)/shard_map/ppermute | solution.py:22
  18.0 11.0 %copy-start.7 = (bf16[128,4096]{1,0:T(8,128)(2,1)S(1)}, bf16[128,4096]{1,0:T(8,128)(2,1)}, u32[]{:S(2)}) copy-start(bf16[128,4096]{1,0:T(8,128)(2,1)} %param.12) | copy-start | bytes 3145732
  19.3 61.5 %all-to-all-start = ((bf16[128,8,512]{2,0,1:T(8,128)(2,1)}), bf16[128,8,512]{2,0,1:T(8,128)(2,1)S(1)}, u32[]{:S(2)}, u32[]{:S(2)}) async-start(bf16[128,8,512]{2,0,1:T(8,128)(2,1)} %copy.50), calls=%async_computation | async-start | bytes 2097152 | tf_op jit(solution)/shard_map/all_to_all | solution.py:54
  22.9 21.1 %collective-permute-start.2 = (bf16[128,512]{0,1:T(8,128)(2,1)}, bf16[128,512]{0,1:T(8,128)(2,1)S(1)}, u32[]{:S(2)}, u32[]{:S(2)}) collective-permute-start(bf16[128,512]{0,1:T(8,128)(2,1)} %get-tuple-element.22), channel_id=1, source_target_pairs={{0,6},{1,7},{2,0},{3,1},{4,2},{5,3},{6,4},{7,5},{8,14},{9,15},{10,... | collective-permute-start | bytes 393224 | tf_op jit(solution)/shard_map/ppermute | solution.py:22
  26.6 20.2 %collective-permute-start.3 = (bf16[128,512]{0,1:T(8,128)(2,1)}, bf16[128,512]{0,1:T(8,128)(2,1)S(1)}, u32[]{:S(2)}, u32[]{:S(2)}) collective-permute-start(bf16[128,512]{0,1:T(8,128)(2,1)} %get-tuple-element.21), channel_id=1, source_target_pairs={{0,5},{1,6},{2,7},{3,0},{4,1},{5,2},{6,3},{7,4},{8,13},{9,14},{10,... | collective-permute-start | bytes 393224 | tf_op jit(solution)/shard_map/ppermute | solution.py:22
  26.6 43.1 %collective-permute-start.4 = (bf16[128,512]{0,1:T(8,128)(2,1)}, bf16[128,512]{0,1:T(8,128)(2,1)}, u32[]{:S(2)}, u32[]{:S(2)}) collective-permute-start(bf16[128,512]{0,1:T(8,128)(2,1)} %get-tuple-element.20), channel_id=1, source_target_pairs={{0,4},{1,5},{2,6},{3,7},{4,0},{5,1},{6,2},{7,3},{8,12},{9,13},{10,... | collective-permute-start | bytes 393224 | tf_op jit(solution)/shard_map/ppermute | solution.py:22
  29.0 42.3 %collective-permute-start.5 = (bf16[128,512]{0,1:T(8,128)(2,1)}, bf16[128,512]{0,1:T(8,128)(2,1)}, u32[]{:S(2)}, u32[]{:S(2)}) collective-permute-start(bf16[128,512]{0,1:T(8,128)(2,1)} %get-tuple-element.19), channel_id=1, source_target_pairs={{0,3},{1,4},{2,5},{3,6},{4,7},{5,0},{6,1},{7,2},{8,11},{9,12},{10,... | collective-permute-start | bytes 393224 | tf_op jit(solution)/shard_map/ppermute | solution.py:22
  30.1 42.8 %collective-permute-start.6 = (bf16[128,512]{0,1:T(8,128)(2,1)}, bf16[128,512]{0,1:T(8,128)(2,1)S(1)}, u32[]{:S(2)}, u32[]{:S(2)}) collective-permute-start(bf16[128,512]{0,1:T(8,128)(2,1)} %get-tuple-element.18), channel_id=1, source_target_pairs={{0,2},{1,3},{2,4},{3,5},{4,6},{5,7},{6,0},{7,1},{8,10},{9,11},{10,... | collective-permute-start | bytes 393224 | tf_op jit(solution)/shard_map/ppermute | solution.py:22
  44.0 29.6 %collective-permute-start.7 = (bf16[128,512]{0,1:T(8,128)(2,1)}, bf16[128,512]{0,1:T(8,128)(2,1)S(1)}, u32[]{:S(2)}, u32[]{:S(2)}) collective-permute-start(bf16[128,512]{0,1:T(8,128)(2,1)} %get-tuple-element.17), channel_id=1, source_target_pairs={{0,1},{1,2},{2,3},{3,4},{4,5},{5,6},{6,7},{7,0},{8,9},{9,10},{10,1... | collective-permute-start | bytes 393224 | tf_op jit(solution)/shard_map/ppermute | solution.py:22
  80.8 7.0 %copy-start.4 = (bf16[128,8,512]{2,0,1:T(8,128)(2,1)}, bf16[128,8,512]{2,0,1:T(8,128)(2,1)S(1)}, u32[]{:S(2)}) copy-start(bf16[128,8,512]{2,0,1:T(8,128)(2,1)S(1)} %all-to-all-done) | copy-start | bytes 3145732
  80.8 11.5 %copy-start.11 = (s32[16,2]{0,1:T(2,128)S(1)}, s32[16,2]{0,1:T(2,128)}, u32[]{:S(2)}) copy-start(s32[16,2]{0,1:T(2,128)} %param.18) | copy-start | bytes 388
  80.8 43.4 %all-to-all-start.1 = ((bf16[128,8,512]{2,0,1:T(8,128)(2,1)}), bf16[128,8,512]{2,0,1:T(8,128)(2,1)}, u32[]{:S(2)}, u32[]{:S(2)}) async-start(bf16[128,8,512]{2,0,1:T(8,128)(2,1)} %bitcast.100), calls=%async_computation.1 | async-start | bytes 2097152 | tf_op jit(solution)/shard_map/all_to_all | solution.py:52
  87.8 9.2 %copy-start.2 = (bf16[1024,512]{0,1:T(8,128)(2,1)}, bf16[1024,512]{0,1:T(8,128)(2,1)S(1)}, u32[]{:S(2)}) copy-start(bf16[1024,512]{0,1:T(8,128)(2,1)S(1)} %constant_dynamic-slice_fusion) | copy-start | bytes 3145732
  87.9 26.3 %collective-permute-start.8 = (bf16[1024,512]{0,1:T(8,128)(2,1)S(1)}, bf16[1024,512]{0,1:T(8,128)(2,1)}, u32[]{:S(2)}, u32[]{:S(2)}) collective-permute-start(bf16[1024,512]{0,1:T(8,128)(2,1)S(1)} %constant_dynamic-slice_fusion), channel_id=1, source_target_pairs={{0,8},{8,16},{16,24},{1,9},{9,17},{17,25},{2,10},{10,18},{18,26},{... | collective-permute-start | bytes 3145736 | tf_op jit(solution)/shard_map/ppermute | solution.py:30
  118.6 26.9 %collective-permute-start = (bf16[1024,512]{0,1:T(8,128)(2,1)}, bf16[1024,512]{0,1:T(8,128)(2,1)}, u32[]{:S(2)}, u32[]{:S(2)}) collective-permute-start(bf16[1024,512]{0,1:T(8,128)(2,1)} %copy.51), channel_id=1, source_target_pairs={{0,8},{8,16},{16,24},{1,9},{9,17},{17,25},{2,10},{10,18},{18,26},{... | collective-permute-start | bytes 3145736 | tf_op jit(solution)/shard_map/ppermute | solution.py:30
  134.4 3.9 copy-start.5
  141.3 4.2 copy-start.3
  153.8 5.9 %copy-start.9 = (s32[128,2]{0,1:T(2,128)S(1)}, s32[128,2]{0,1:T(2,128)}, u32[]{:S(2)}) copy-start(s32[128,2]{0,1:T(2,128)} %param.16) | copy-start | bytes 3076
  155.1 31.1 %all-to-all-start.2 = ((bf16[8,128,512]{2,1,0:T(8,128)(2,1)}), bf16[8,128,512]{2,1,0:T(8,128)(2,1)S(1)}, u32[]{:S(2)}, u32[]{:S(2)}) async-start(bf16[8,128,512]{2,1,0:T(8,128)(2,1)} %bitcast.23), calls=%async_computation.2 | async-start | bytes 2097152 | tf_op jit(solution)/shard_map/all_to_all | solution.py:101
  159.6 173.9 %all-gather.2.cloned.1.call-start = ((), (), s32[]{:S(2)}) async-start(), calls=%async_computation.6 | async-start | bytes 10485760 | tf_op jit(solution)/shard_map/all_gather | solution.py:125
  186.5 1.2 copy-start
  186.7 1.5 copy-start.8
  245.1 210.6 %reduce-scatter.2.cloned.1.call-start = ((), (), s32[]{:S(2)}) async-start(), calls=%async_computation.7 | async-start | bytes 10485760 | tf_op jit(solution)/shard_map/reduce_scatter | solution.py:133
  333.6 12.7 %copy-start.12 = (bf16[32,32,4096]{2,1,0:T(8,128)(2,1)S(1)}, bf16[32,32,4096]{2,1,0:T(8,128)(2,1)}, u32[]{:S(2)}) copy-start(bf16[32,32,4096]{2,1,0:T(8,128)(2,1)} %all-gather.2.cloned.1.call-done) | copy-start | bytes 25165828
  333.6 24.7 %slice-start = ((s8[8388608]{0:T(1024)(128)(4,1)}), s8[4194304]{0:T(1024)(128)(4,1)S(1)}, s32[]{:S(2)}) async-start(s8[8388608]{0:T(1024)(128)(4,1)} %bitcast.119), calls=%async_computation.8 | async-start | bytes 8388608
  346.3 12.0 %slice-start.1 = ((s8[8388608]{0:T(1024)(128)(4,1)}), s8[4194304]{0:T(1024)(128)(4,1)S(1)}, s32[]{:S(2)}) async-start(s8[8388608]{0:T(1024)(128)(4,1)} %bitcast.119), calls=%async_computation.9 | async-start | bytes 8388608
  369.3 91.4 %copy-start.10 = (f32[128,2]{0,1:T(2,128)S(1)}, f32[128,2]{0,1:T(2,128)}, u32[]{:S(2)}) copy-start(f32[128,2]{0,1:T(2,128)} %param.17) | copy-start | bytes 3076
  455.8 54.0 %all-to-all-start.4 = ((bf16[8,32,4096]{2,1,0:T(8,128)(2,1)}), bf16[8,32,4096]{2,1,0:T(8,128)(2,1)}, u32[]{:S(2)}, u32[]{:S(2)}) async-start(bf16[8,32,4096]{2,1,0:T(8,128)(2,1)} %reduce-scatter.2.cloned.1.call-done), calls=%async_computation.5 | async-start | bytes 4194304 | tf_op jit(solution)/shard_map/all_to_all | solution.py:136
  527.4 8.8 %copy-start.1 = (bf16[128,4096]{1,0:T(8,128)(2,1)S(1)}, bf16[128,4096]{1,0:T(8,128)(2,1)}, u32[]{:S(2)}) copy-start(bf16[128,4096]{1,0:T(8,128)(2,1)} %param.11) | copy-start | bytes 3145732
Sparse Core Ops, SparseCore 0:
  245.3 88.2 all-gather.1
  369.4 86.3 reduce-scatter.1
